TPU v7x, 32 devices: a whole 2x2x4 slice. The times are simulated.
32 devices in a mesh: space: 8 (over z, y), band: 4 (over x, core).
Axes of the slice: x: 2, y: 2, z: 4, core: 2. Of those that a mesh axis runs over, the one named last changes fastest.
Arguments:
- columns: float32 [16, 48, 32, 128], P('band', 'space'), may hold values from -6 to 6
- potential: float32 [48, 32, 128], P('space'), may hold values from -1 to 3
- orbitals: float32 [512, 48, 32, 128], P('band', 'space'), may hold values from -0.0546875 to 0.0546875
Outputs:
- projected: float32 [16, 48, 32, 128], P('band', 'space')
- correlation: float32 [512, 16], P('band')
All inputs are finite; a program needn't handle non-finite values.
Results may differ from a plain program's by a relative error of at most 0.00011.
Values sent between devices are 32-bit elements; how exact they have to be, the bound alone decides.
No kernel may reach another device: no remote copies, remote signals or barrier semaphores. Data moves between devices by JAX's collectives and lax.ppermute only.
A program may use at most 128 MiB of HBM per device.

v0:
```python
import jax
import jax.numpy as jnp
from jax import lax
from jax.sharding import PartitionSpec as P

COEFFS = (
    -5369.0 / 1800.0,
    12.0 / 7.0,
    -15.0 / 56.0,
    10.0 / 189.0,
    -1.0 / 112.0,
    2.0 / 1925.0,
    -1.0 / 16632.0,
)


def padded_2(array, sides, width):
    for axis, dim in sides:
        size, length = (lax.axis_size(axis), array.shape[dim])
        up = [(i, (i + 1) % size) for i in range(size)]
        down = [(j, i) for i, j in up]
        last = lax.slice_in_dim(array, length - width, length, axis=dim)
        first = lax.slice_in_dim(array, 0, width, axis=dim)
        before = lax.ppermute(last, axis, up)
        after = lax.ppermute(first, axis, down)
        array = jnp.concatenate([before, array, after], axis=dim)
    return array


def hamiltonian(values, potential):
    padded = padded_2(values, (("space", 1),), 6)
    planes = values.shape[1]
    laplace = 3.0 * COEFFS[0] * values
    for offset in range(1, 7):
        along = (
            padded[:, 6 + offset : 6 + offset + planes]
            + padded[:, 6 - offset : 6 - offset + planes]
        )
        along = along + jnp.roll(values, offset, 2) + jnp.roll(values, -offset, 2)
        along = along + jnp.roll(values, offset, 3) + jnp.roll(values, -offset, 3)
        laplace = laplace + COEFFS[offset] * along
    return -0.5 * laplace + potential[None] * values


def shards(columns, potential, orbitals):
    applied = hamiltonian(columns, potential)
    orb_local = orbitals.shape[0]
    col_local = applied.shape[0]
    psi_flat = orbitals.reshape(orb_local, -1)
    piece = lax.all_gather(applied, "band", axis=0, tiled=True)
    partial_correlation = jnp.einsum(
        "oc,kc->ok", psi_flat, piece.reshape(piece.shape[0], -1), precision=lax.Precision.HIGHEST
    )
    correlation = lax.psum(partial_correlation, "space")
    removed = jnp.einsum("ok,oc->kc", correlation, psi_flat, precision=lax.Precision.HIGHEST)
    removed_all = lax.psum_scatter(
        removed.reshape((col_local * lax.axis_size("band"),) + applied.shape[1:]),
        "band",
        scatter_dimension=0,
        tiled=True,
    )
    projected = applied - removed_all
    return (projected, correlation)


def solution(mesh):
    placed = (
        P("band", "space", None, None),
        P("space", None, None),
        P("band", "space", None, None),
    )
    return jax.shard_map(
        shards,
        mesh=mesh,
        in_specs=placed,
        out_specs=(P("band", "space", None, None), P("band", None)),
        check_vma=False,
    )
```

profile of v0, /device:TPU:0, one launch (start us, length us, event | category | flops | bytes accessed | tf_op | source)
XLA Modules:
  0.0 155.2 jit_solution(5152359355266835999)
XLA Ops:
  7.2 3.0 %collective-permute-start.1 = (f32[4,6,32,128]{3,2,1,0:T(8,128)}, f32[4,6,32,128]{3,2,1,0:T(8,128)S(1)}, u32[]{:S(2)}, u32[]{:S(2)}) collective-permute-start(f32[4,6,32,128]{3,2,1,0:T(8,128)} %param.3), channel_id=1, source_target_pairs={{0,4},{4,8},{8,12},{12,16},{16,20},{20,24},{24,28},{28,0},{1,5},{5... | collective-permute-start | bytes 1179656 | tf_op jit(solution)/shard_map/ppermute | solution.py:24
  10.3 3.1 %collective-permute-start = (f32[4,6,32,128]{3,2,1,0:T(8,128)}, f32[4,6,32,128]{3,2,1,0:T(8,128)S(1)}, u32[]{:S(2)}, u32[]{:S(2)}) collective-permute-start(f32[4,6,32,128]{3,2,1,0:T(8,128)} %param.3), channel_id=1, source_target_pairs={{4,0},{8,4},{12,8},{16,12},{20,16},{24,20},{28,24},{0,28},{5,1},{9... | collective-permute-start | bytes 1179656 | tf_op jit(solution)/shard_map/ppermute | solution.py:25
  13.4 1.3 fusion.69
  14.6 1.4 fusion.67
  16.0 1.4 fusion.68
  17.4 1.3 fusion.65
  18.6 1.4 fusion.63
  20.0 1.4 fusion.64
  21.4 1.3 fusion.61
  22.6 1.0 fusion.62
  23.6 1.4 fusion.59
  25.4 0.2 fusion.56
  26.6 0.8 collective-permute-done.1
  27.5 2.0 %collective-permute-done = f32[4,6,32,128]{3,2,1,0:T(8,128)S(1)} collective-permute-done((f32[4,6,32,128]{3,2,1,0:T(8,128)}, f32[4,6,32,128]{3,2,1,0:T(8,128)S(1)}, u32[]{:S(2)}, u32[]{:S(2)}) %collective-permute-start) | collective-permute-done | bytes 393248 | tf_op jit(solution)/shard_map/ppermute | solution.py:25
  29.5 3.8 %fusion.16 = f32[4,6,32,128]{3,2,1,0:T(8,128)} fusion(f32[4,12,32,128]{3,2,1,0:T(8,128)S(1)} %get-tuple-element.53, f32[4,12,32,128]{3,2,1,0:T(8,128)S(1)} %constant_dynamic-update-slice_fusion, f32[4,6,31,128]{3,2,1,0:T(8,128)S(1)} %get-tuple-element.49, f32[4,6,1,128]{3,2,1,0:T(1,128)S(1)} %get-tuple-element.51, ...), kind=kLoop, calls=%fused_computation.14 | loop fusion | flops 6881280 | bytes 15040512 | tf_op jit(solution)/shard_map/add | solution.py:42
  33.3 0.2 reduce-scatter.2.cloned.1.call-start
  33.6 18.9 %copy.78 = f32[16,8,192,128]{3,1,2,0:T(8,128)} copy(f32[16,8,192,128]{3,2,1,0:T(8,128)} %bitcast.21) | data formatting | bytes 25165824
  52.5 12.6 %copy.64 = f32[24576,128]{1,0:T(8,128)} copy(f32[24576,128]{0,1:T(8,128)} %bitcast.23) | data formatting | bytes 25165824 | tf_op jit(solution)/shard_map/ok,oc->kc/dot_general | solution.py:55
  65.1 20.7 %fusion.3 = f32[128,16]{0,1:T(8,128)S(1)} fusion(f32[128,6,32,128]{3,2,1,0:T(8,128)} %param.5, f32[16,6,32,128]{3,2,1,0:T(8,128)} %all-gather.2.cloned.1.call-done), kind=kOutput, calls=%fused_computation.4 | convolution fusion | flops 603979776 | bytes 14163968 | tf_op jit(solution)/shard_map/oc,kc->ok/dot_general | solution.py:51
  85.8 21.0 %psum.7 = f32[128,16]{0,1:T(8,128)S(1)} all-reduce(f32[128,16]{0,1:T(8,128)S(1)} %fusion.3), channel_id=1, replica_groups=mesh['space'=8,'band'=4] {'space'}, use_global_device_ids=true, to_apply=%region_0.1 | all-reduce | flops 2048 | bytes 16384 | tf_op jit(solution)/shard_map/psum | solution.py:54
  106.7 12.7 %fusion.45 = f32[16,6,32,128]{3,0,2,1:T(8,128)S(1)} fusion(f32[6,32,128,128]{3,2,1,0:T(8,128)} %bitcast.22, f32[128,16]{0,1:T(8,128)S(1)} %psum.7), kind=kOutput, calls=%fused_computation.52 | convolution fusion | flops 603979776 | bytes 14163968 | tf_op jit(solution)/shard_map/ok,oc->kc/dot_general | solution.py:55
  119.5 1.7 %copy.65 = f32[16,6,32,128]{3,2,1,0:T(8,128)} copy(f32[16,6,32,128]{3,0,2,1:T(8,128)S(1)} %fusion.45) | data formatting | bytes 3145728 | tf_op jit(solution)/shard_map/ok,oc->kc/dot_general | solution.py:55
  121.2 25.4 %reduce-scatter.2.cloned.1.call-done = f32[4,6,32,128]{3,2,1,0:T(8,128)} async-done(((f32[16,6,32,128]{3,2,1,0:T(8,128)}), f32[4,6,32,128]{3,2,1,0:T(8,128)}) %reduce-scatter.2.cloned.1.call-update) | async-done | bytes 393232 | tf_op jit(solution)/shard_map/reduce_scatter | solution.py:56
  146.6 1.8 %sub.3 = f32[4,6,32,128]{3,2,1,0:T(8,128)} subtract(f32[4,6,32,128]{3,2,1,0:T(8,128)S(1)} %copy-done.1, f32[4,6,32,128]{3,2,1,0:T(8,128)} %reduce-scatter.2.cloned.1.call-done) | non-fusion elementwise | flops 98304 | bytes 1179648 | tf_op jit(solution)/shard_map/sub | solution.py:62
  (29 shorter events, 1.6 us)
Async XLA Ops:
  7.2 17.8 %copy-start = (f32[4,6,32,128]{3,2,1,0:T(8,128)S(1)}, f32[4,6,32,128]{3,2,1,0:T(8,128)}, u32[]{:S(2)}) copy-start(f32[4,6,32,128]{3,2,1,0:T(8,128)} %param.3) | copy-start | bytes 1179652
  7.2 57.9 %all-gather.2.cloned.1.call-start = ((), (), s32[]{:S(2)}) async-start(), calls=%async_computation.1 | async-start | bytes 1966080 | tf_op jit(solution)/shard_map/all_gather | solution.py:50
  7.2 20.2 %collective-permute-start.1 = (f32[4,6,32,128]{3,2,1,0:T(8,128)}, f32[4,6,32,128]{3,2,1,0:T(8,128)S(1)}, u32[]{:S(2)}, u32[]{:S(2)}) collective-permute-start(f32[4,6,32,128]{3,2,1,0:T(8,128)} %param.3), channel_id=1, source_target_pairs={{0,4},{4,8},{8,12},{12,16},{16,20},{20,24},{24,28},{28,0},{1,5},{5... | collective-permute-start | bytes 1179656 | tf_op jit(solution)/shard_map/ppermute | solution.py:24
  10.3 19.2 %collective-permute-start = (f32[4,6,32,128]{3,2,1,0:T(8,128)}, f32[4,6,32,128]{3,2,1,0:T(8,128)S(1)}, u32[]{:S(2)}, u32[]{:S(2)}) collective-permute-start(f32[4,6,32,128]{3,2,1,0:T(8,128)} %param.3), channel_id=1, source_target_pairs={{4,0},{8,4},{12,8},{16,12},{20,16},{24,20},{28,24},{0,28},{5,1},{9... | collective-permute-start | bytes 1179656 | tf_op jit(solution)/shard_map/ppermute | solution.py:25
  20.0 9.5 %copy-start.2 = (f32[6,32,128]{2,1,0:T(8,128)S(1)}, f32[6,32,128]{2,1,0:T(8,128)}, u32[]{:S(2)}) copy-start(f32[6,32,128]{2,1,0:T(8,128)} %param.4) | copy-start | bytes 294916
  33.3 113.2 %reduce-scatter.2.cloned.1.call-start = ((), (), s32[]{:S(2)}) async-start(), calls=%async_computation.2 | async-start | bytes 1966080 | tf_op jit(solution)/shard_map/reduce_scatter | solution.py:56
  85.7 60.8 %copy-start.1 = (f32[4,6,32,128]{3,2,1,0:T(8,128)S(1)}, f32[4,6,32,128]{3,2,1,0:T(8,128)}, u32[]{:S(2)}) copy-start(f32[4,6,32,128]{3,2,1,0:T(8,128)} %fusion.16) | copy-start | bytes 1179652
  106.7 41.6 %copy-start.3 = (f32[128,16]{0,1:T(8,128)}, f32[128,16]{0,1:T(8,128)S(1)}, u32[]{:S(2)}) copy-start(f32[128,16]{0,1:T(8,128)S(1)} %psum.7) | copy-start | bytes 24580
Sparse Core Ops, SparseCore 0:
  33.5 19.7 all-gather.1
  121.3 25.2 reduce-scatter.1
where the time goes:
time: 156 us; the launch traced here: 155 us
  local copies, waits for them, and re-layouts  46.5 us (30%)
  matrix products  33.4 us (21%)
  waiting for transfers between devices  28.2 us (18%)
  blocking collectives  21 us (13%)
  between operations  14.2 us (9%)
  starting transfers between devices  6.41 us (4%)
  other arithmetic  5.59 us (4%)
    reduce_scatter x1, waiting for transfers between devices, shards(): lax.psum_scatter(removed.reshape((col_local * lax.axis_size('band'),) + a...  25.4 us
    psum x1, blocking collectives, shards(): correlation = lax.psum(partial_correlation, 'space')  21 us
    dot_general x1, matrix products, shards(): jnp.einsum('oc,kc->ok', psi_flat, piece.reshape(piece.shape[0], -1), prec...  20.7 us
    unnamed x11, local copies, waits for them, and re-layouts  19 us
    dot_general x2, local copies, waits for them, and re-layouts, shards(): jnp.einsum('ok,oc->kc', correlation, psi_flat, precision=lax.Precision.HI...  14.3 us
    dot_general x1, matrix products, shards(): jnp.einsum('ok,oc->kc', correlation, psi_flat, precision=lax.Precision.HI...  12.7 us
    slice x12, local copies, waits for them, and re-layouts, hamiltonian(): along = along + jnp.roll(values, offset, 3) + jnp.roll(values, -offset, 3)  8.09 us
    slice x12, local copies, waits for them, and re-layouts, hamiltonian(): along = along + jnp.roll(values, offset, 2) + jnp.roll(values, -offset, 2)  5.05 us
  transfers between devices with their start and end apart: 4, of which 3 were waited for; matrix products, arithmetic and copies ran while one was open for 29% of the time, Pallas kernels for 0%

commit v1 on v0

--- a/solution.py
+++ b/solution.py
@@ -51,7 +51,7 @@
     partial_correlation = jnp.einsum(
         "oc,kc->ok", psi_flat, piece.reshape(piece.shape[0], -1), precision=lax.Precision.HIGHEST
     )
-    correlation = lax.psum(partial_correlation, "space")
+    correlation = jnp.sum(lax.all_gather(partial_correlation, "space"), axis=0)
     removed = jnp.einsum("ok,oc->kc", correlation, psi_flat, precision=lax.Precision.HIGHEST)
     removed_all = lax.psum_scatter(
         removed.reshape((col_local * lax.axis_size("band"),) + applied.shape[1:]),

time: 156 us -> 167 us (1.071)
  blocking collectives: 21 us -> 30.9 us
  waiting for transfers between devices: 28.2 us -> 31.1 us
  matrix products: 33.4 us -> 31.2 us
    all_gather x0 -> x1, blocking collectives: none -> 30.9 us  [shards(): correlation = jnp.sum(lax.all_gather(partial_correlation, 'space'), axis=0)]
    psum x1 -> x0, blocking collectives: 21 us -> none  [shards(): correlation = lax.psum(partial_correlation, 'space')]
    reduce_scatter x1, waiting for transfers between devices: 25.4 us -> 28.3 us  [shards(): lax.psum_scatter(removed.reshape((col_local * lax.axis_size('band'),) + a...]
    dot_general x1, matrix products: 12.7 us -> 10.5 us  [shards(): jnp.einsum('ok,oc->kc', correlation, psi_flat, precision=lax.Precision.HI...]
    unnamed x11 -> x14, local copies, waits for them, and re-layouts: 19 us -> 19.1 us
  transfers between devices with their start and end apart: 4 -> 4, of which waited for: 3 -> 3; matrix products, arithmetic and copies ran while one was open for 29% -> 27% of each run, Pallas kernels for 0% -> 0%
where the time goes in v1:
time: 167 us; the launch traced here: 166 us
  local copies, waits for them, and re-layouts  46.5 us (28%)
  matrix products  31.2 us (19%)
  waiting for transfers between devices  31.1 us (19%)
  blocking collectives  30.9 us (19%)
  between operations  14.2 us (9%)
  starting transfers between devices  6.41 us (4%)
  other arithmetic  5.61 us (3%)
    all_gather x1, blocking collectives, shards(): correlation = jnp.sum(lax.all_gather(partial_correlation, 'space'), axis=0)  30.9 us
    reduce_scatter x1, waiting for transfers between devices, shards(): lax.psum_scatter(removed.reshape((col_local * lax.axis_size('band'),) + a...  28.3 us
    dot_general x1, matrix products, shards(): jnp.einsum('oc,kc->ok', psi_flat, piece.reshape(piece.shape[0], -1), prec...  20.8 us
    unnamed x14, local copies, waits for them, and re-layouts  19.1 us
    dot_general x2, local copies, waits for them, and re-layouts, shards(): jnp.einsum('ok,oc->kc', correlation, psi_flat, precision=lax.Precision.HI...  14.3 us
    dot_general x1, matrix products, shards(): jnp.einsum('ok,oc->kc', correlation, psi_flat, precision=lax.Precision.HI...  10.5 us
    slice x12, local copies, waits for them, and re-layouts, hamiltonian(): along = along + jnp.roll(values, offset, 3) + jnp.roll(values, -offset, 3)  8.09 us
    slice x12, local copies, waits for them, and re-layouts, hamiltonian(): along = along + jnp.roll(values, offset, 2) + jnp.roll(values, -offset, 2)  5.05 us
  transfers between devices with their start and end apart: 4, of which 3 were waited for; matrix products, arithmetic and copies ran while one was open for 27% of the time, Pallas kernels for 0%

profile of v1, /device:TPU:0, one launch (start us, length us, event | category | flops | bytes accessed | tf_op | source)
XLA Modules:
  0.0 166.1 jit_solution(3599535021645321383)
XLA Ops:
  7.2 3.0 %collective-permute-start.1 = (f32[4,6,32,128]{3,2,1,0:T(8,128)}, f32[4,6,32,128]{3,2,1,0:T(8,128)S(1)}, u32[]{:S(2)}, u32[]{:S(2)}) collective-permute-start(f32[4,6,32,128]{3,2,1,0:T(8,128)} %param.3), channel_id=1, source_target_pairs={{0,4},{4,8},{8,12},{12,16},{16,20},{20,24},{24,28},{28,0},{1,5},{5... | collective-permute-start | bytes 1179656 | tf_op jit(solution)/shard_map/ppermute | solution.py:24
  10.3 3.1 %collective-permute-start = (f32[4,6,32,128]{3,2,1,0:T(8,128)}, f32[4,6,32,128]{3,2,1,0:T(8,128)S(1)}, u32[]{:S(2)}, u32[]{:S(2)}) collective-permute-start(f32[4,6,32,128]{3,2,1,0:T(8,128)} %param.3), channel_id=1, source_target_pairs={{4,0},{8,4},{12,8},{16,12},{20,16},{24,20},{28,24},{0,28},{5,1},{9... | collective-permute-start | bytes 1179656 | tf_op jit(solution)/shard_map/ppermute | solution.py:25
  13.4 1.3 fusion.69
  14.6 1.4 fusion.67
  16.0 1.4 fusion.68
  17.4 1.3 fusion.65
  18.6 1.4 fusion.63
  20.0 1.4 fusion.64
  21.4 1.3 fusion.61
  22.6 1.0 fusion.62
  23.6 1.4 fusion.59
  25.4 0.2 fusion.56
  26.6 0.8 collective-permute-done.1
  27.5 2.0 %collective-permute-done = f32[4,6,32,128]{3,2,1,0:T(8,128)S(1)} collective-permute-done((f32[4,6,32,128]{3,2,1,0:T(8,128)}, f32[4,6,32,128]{3,2,1,0:T(8,128)S(1)}, u32[]{:S(2)}, u32[]{:S(2)}) %collective-permute-start) | collective-permute-done | bytes 393248 | tf_op jit(solution)/shard_map/ppermute | solution.py:25
  29.5 3.8 %fusion.16 = f32[4,6,32,128]{3,2,1,0:T(8,128)} fusion(f32[4,12,32,128]{3,2,1,0:T(8,128)S(1)} %get-tuple-element.53, f32[4,12,32,128]{3,2,1,0:T(8,128)S(1)} %constant_dynamic-update-slice_fusion, f32[4,6,31,128]{3,2,1,0:T(8,128)S(1)} %get-tuple-element.49, f32[4,6,1,128]{3,2,1,0:T(1,128)S(1)} %get-tuple-element.51, ...), kind=kLoop, calls=%fused_computation.14 | loop fusion | flops 6881280 | bytes 15040512 | tf_op jit(solution)/shard_map/add | solution.py:42
  33.3 0.2 reduce-scatter.2.cloned.1.call-start
  33.6 18.9 %copy.79 = f32[16,8,192,128]{3,1,2,0:T(8,128)} copy(f32[16,8,192,128]{3,2,1,0:T(8,128)} %bitcast.26) | data formatting | bytes 25165824
  52.5 12.6 %copy.64 = f32[24576,128]{1,0:T(8,128)} copy(f32[24576,128]{0,1:T(8,128)} %bitcast.28) | data formatting | bytes 25165824 | tf_op jit(solution)/shard_map/ok,oc->kc/dot_general | solution.py:55
  65.1 20.8 %fusion.3 = f32[128,16]{0,1:T(8,128)S(1)} fusion(f32[128,6,32,128]{3,2,1,0:T(8,128)} %param.5, f32[16,6,32,128]{3,2,1,0:T(8,128)} %all-gather.3.cloned.1.call-done), kind=kOutput, calls=%fused_computation.4 | convolution fusion | flops 603979776 | bytes 14163968 | tf_op jit(solution)/shard_map/oc,kc->ok/dot_general | solution.py:51
  85.9 30.9 %all-gather = f32[1024,16]{0,1:T(8,128)S(1)} all-gather(f32[128,16]{0,1:T(8,128)S(1)} %fusion.3), channel_id=2, replica_groups=mesh['space'=8,'band'=4] {'space'}, dimensions={0}, use_global_device_ids=true | all-gather | bytes 73728 | tf_op jit(solution)/shard_map/all_gather | solution.py:54
  116.9 10.5 %fusion.45 = f32[16,6,32,128]{3,0,2,1:T(8,128)S(1)} fusion(f32[6,32,128,128]{3,2,1,0:T(8,128)S(1)} %bitcast.27, f32[128,16]{0,1:T(8,128)S(1)} %bitcast_reduce_fusion), kind=kOutput, calls=%fused_computation.53 | convolution fusion | flops 603979776 | bytes 14163968 | tf_op jit(solution)/shard_map/ok,oc->kc/dot_general | solution.py:55
  127.4 1.7 %copy.65 = f32[16,6,32,128]{3,2,1,0:T(8,128)} copy(f32[16,6,32,128]{3,0,2,1:T(8,128)S(1)} %fusion.45) | data formatting | bytes 3145728 | tf_op jit(solution)/shard_map/ok,oc->kc/dot_general | solution.py:55
  129.1 28.3 %reduce-scatter.2.cloned.1.call-done = f32[4,6,32,128]{3,2,1,0:T(8,128)} async-done(((f32[16,6,32,128]{3,2,1,0:T(8,128)}), f32[4,6,32,128]{3,2,1,0:T(8,128)}) %reduce-scatter.2.cloned.1.call-update) | async-done | bytes 393232 | tf_op jit(solution)/shard_map/reduce_scatter | solution.py:56
  157.4 1.8 %sub.3 = f32[4,6,32,128]{3,2,1,0:T(8,128)} subtract(f32[4,6,32,128]{3,2,1,0:T(8,128)S(1)} %copy-done.2, f32[4,6,32,128]{3,2,1,0:T(8,128)} %reduce-scatter.2.cloned.1.call-done) | non-fusion elementwise | flops 98304 | bytes 1179648 | tf_op jit(solution)/shard_map/sub | solution.py:62
  (33 shorter events, 1.7 us)
Async XLA Ops:
  7.2 17.8 %copy-start = (f32[4,6,32,128]{3,2,1,0:T(8,128)S(1)}, f32[4,6,32,128]{3,2,1,0:T(8,128)}, u32[]{:S(2)}) copy-start(f32[4,6,32,128]{3,2,1,0:T(8,128)} %param.3) | copy-start | bytes 1179652
  7.2 57.9 %all-gather.3.cloned.1.call-start = ((), (), s32[]{:S(2)}) async-start(), calls=%async_computation.1 | async-start | bytes 1966080 | tf_op jit(solution)/shard_map/all_gather | solution.py:50
  7.2 20.2 %collective-permute-start.1 = (f32[4,6,32,128]{3,2,1,0:T(8,128)}, f32[4,6,32,128]{3,2,1,0:T(8,128)S(1)}, u32[]{:S(2)}, u32[]{:S(2)}) collective-permute-start(f32[4,6,32,128]{3,2,1,0:T(8,128)} %param.3), channel_id=1, source_target_pairs={{0,4},{4,8},{8,12},{12,16},{16,20},{20,24},{24,28},{28,0},{1,5},{5... | collective-permute-start | bytes 1179656 | tf_op jit(solution)/shard_map/ppermute | solution.py:24
  10.3 19.2 %collective-permute-start = (f32[4,6,32,128]{3,2,1,0:T(8,128)}, f32[4,6,32,128]{3,2,1,0:T(8,128)S(1)}, u32[]{:S(2)}, u32[]{:S(2)}) collective-permute-start(f32[4,6,32,128]{3,2,1,0:T(8,128)} %param.3), channel_id=1, source_target_pairs={{4,0},{8,4},{12,8},{16,12},{20,16},{24,20},{28,24},{0,28},{5,1},{9... | collective-permute-start | bytes 1179656 | tf_op jit(solution)/shard_map/ppermute | solution.py:25
  20.0 9.5 %copy-start.3 = (f32[6,32,128]{2,1,0:T(8,128)S(1)}, f32[6,32,128]{2,1,0:T(8,128)}, u32[]{:S(2)}) copy-start(f32[6,32,128]{2,1,0:T(8,128)} %param.4) | copy-start | bytes 294916
  33.3 124.1 %reduce-scatter.2.cloned.1.call-start = ((), (), s32[]{:S(2)}) async-start(), calls=%async_computation.2 | async-start | bytes 1966080 | tf_op jit(solution)/shard_map/reduce_scatter | solution.py:56
  65.1 51.8 %copy-start.1 = (f32[24576,128]{1,0:T(8,128)S(1)}, f32[24576,128]{1,0:T(8,128)}, u32[]{:S(2)}) copy-start(f32[24576,128]{1,0:T(8,128)} %copy.64) | copy-start | bytes 37748740
  85.9 71.5 %copy-start.2 = (f32[4,6,32,128]{3,2,1,0:T(8,128)S(1)}, f32[4,6,32,128]{3,2,1,0:T(8,128)}, u32[]{:S(2)}) copy-start(f32[4,6,32,128]{3,2,1,0:T(8,128)} %fusion.16) | copy-start | bytes 1179652
  116.9 42.3 %copy-start.4 = (f32[128,16]{0,1:T(8,128)}, f32[128,16]{0,1:T(8,128)S(1)}, u32[]{:S(2)}) copy-start(f32[128,16]{0,1:T(8,128)S(1)} %bitcast_reduce_fusion) | copy-start | bytes 24580
Sparse Core Ops, SparseCore 0:
  33.5 19.7 all-gather.2
  129.2 28.1 reduce-scatter.1
